TPU v7x, 32 devices: a whole 2x2x4 slice. The times are simulated.
32 devices in a mesh: obs: 8 (over z, core), state: 4 (over y, x).
Axes of the slice: x: 2, y: 2, z: 4, core: 2. Of those that a mesh axis runs over, the one named last changes fastest.
Arguments:
- ensemble: bfloat16 [4, 1024, 256], P('state'), may hold values from -16 to 16
- obs_values: float32 [16384], P('obs'), may hold values from -72 to 72
- obs_error: float32 [16384], P('obs'), may hold values from 6 to 24
- h_blocks: bfloat16 [8, 4, 64, 128, 128], P('obs', 'state'), may hold values from -0.125 to 0.125
- block_rows: int32 [8, 4, 64], P('obs', 'state'), may hold values from 0 to 15
- block_cols: int32 [8, 4, 64], P('obs', 'state'), may hold values from 0 to 7
- block_count: int32 [8, 4], P('obs', 'state'), may hold values from 32 to 64, as said below
Outputs:
- analysis: bfloat16 [4, 1024, 256], P('state', 'obs')
Inputs may be any that keep to these rules, and one draw needn't show every extreme that they name: `block_count`: some device has exactly 64 live slots in every draw.
All inputs are finite; a program needn't handle non-finite values.
Results may differ from a plain program's by a relative error of at most 0.009.
Values sent between devices are 32-bit elements; how exact they have to be, the bound alone decides.
A program may use at most 64 MiB of HBM per device.

v0:
```python
import math
import jax
import jax.numpy as jnp
from jax import lax
from jax.sharding import PartitionSpec as P

K = 256
BS = 128
M_DEV = 2048
BLK_DEV = 64


def on_device(ensemble, obs_values, obs_error, h_blocks, block_rows, block_cols, block_count):
    members = ensemble[0]
    slab_rows = members.shape[0]
    state_blocks = slab_rows // BS
    obs_blocks = M_DEV // BS
    member_blocks = members.reshape(state_blocks, BS, K)
    group_size = math.gcd(BLK_DEV, 32)
    group_count = BLK_DEV // group_size
    all_blocks = h_blocks[0, 0]
    all_cols = block_cols[0, 0]
    all_rows = block_rows[0, 0]
    live_count = block_count[0, 0]
    block_ids = jnp.arange(obs_blocks, dtype=jnp.int32)

    def add_group(group_index, carry):
        start = (group_index * group_size).astype(jnp.int32)
        blocks = lax.dynamic_slice_in_dim(all_blocks, start, group_size, 0)
        cols = lax.dynamic_slice_in_dim(all_cols, start, group_size, 0)
        rows = lax.dynamic_slice_in_dim(all_rows, start, group_size, 0)
        live_mask = start + jnp.arange(group_size, dtype=jnp.int32) < live_count
        picked = member_blocks[cols]
        products = jnp.einsum("bij,bjk->bik", blocks, picked, preferred_element_type=jnp.float32)
        upper_part = products.astype(jnp.bfloat16)
        lower_part = (products - upper_part.astype(jnp.float32)).astype(jnp.bfloat16)
        onehot = ((rows[None, :] == block_ids[:, None]) & live_mask[None, :]).astype(jnp.bfloat16)
        carry = carry + jnp.einsum(
            "mb,bik->mik", onehot, upper_part, preferred_element_type=jnp.float32
        )
        carry = carry + jnp.einsum(
            "mb,bik->mik", onehot, lower_part, preferred_element_type=jnp.float32
        )
        return carry

    accumulated = lax.fori_loop(
        0, group_count, add_group, jnp.zeros((obs_blocks, BS, K), jnp.float32)
    )
    slab_term = accumulated.reshape(M_DEV, K)
    state_devices = lax.axis_size("state")
    rows_share = M_DEV // state_devices
    row_offset = lax.axis_index("state") * rows_share
    own_rows = lax.psum_scatter(slab_term, "state", scatter_dimension=0, tiled=True)
    own_values = lax.dynamic_slice_in_dim(obs_values, row_offset, rows_share, 0)
    own_errors = lax.dynamic_slice_in_dim(obs_error, row_offset, rows_share, 0)
    obs_mean = jnp.mean(own_rows, axis=1)
    whitened = (own_rows - obs_mean[:, None]) / own_errors[:, None]
    innovation = (own_values - obs_mean) / own_errors
    gram_part = lax.dot_general(
        whitened, whitened, (((0,), (0,)), ((), ())), precision=lax.Precision.HIGHEST
    )
    projected_part = jnp.dot(innovation, whitened, precision=lax.Precision.HIGHEST)
    identity = jnp.eye(K, dtype=jnp.float32)
    gram_sum, projected_innovation = lax.psum((gram_part, projected_part), ("obs", "state"))
    lower_factor = jnp.linalg.cholesky(gram_sum + (K - 1) * identity)
    halfway = lax.linalg.triangular_solve(
        lower_factor, projected_innovation[:, None], left_side=True, lower=True
    )
    mean_weight = lax.linalg.triangular_solve(
        lower_factor, halfway, left_side=True, lower=True, transpose_a=True
    )
    root_inverse = lax.linalg.triangular_solve(
        lower_factor, identity, left_side=True, lower=True, transpose_a=True
    )
    transform = (math.sqrt(K - 1) * root_inverse + mean_weight).astype(jnp.bfloat16)
    piece_rows = slab_rows // lax.axis_size("obs")
    own_piece = lax.dynamic_slice_in_dim(
        members, lax.axis_index("obs") * piece_rows, piece_rows, 0
    ).astype(jnp.float32)
    state_mean = jnp.mean(own_piece, axis=1)
    anomalies = (own_piece - state_mean[:, None]).astype(jnp.bfloat16)
    analysis = state_mean[:, None] + jnp.dot(
        anomalies, transform, preferred_element_type=jnp.float32
    )
    return analysis.astype(jnp.bfloat16)[None]


def solution(mesh):
    placed = (
        P("state", None, None),
        P("obs"),
        P("obs"),
        P("obs", "state", None, None, None),
        P("obs", "state", None),
        P("obs", "state", None),
        P("obs", "state"),
    )
    return jax.shard_map(
        on_device, mesh=mesh, in_specs=placed, out_specs=P("state", "obs", None), check_vma=False
    )
```

profile of v0, /device:TPU:0, one launch (start us, length us, event | category | flops | bytes accessed | tf_op | source)
XLA Modules:
  0.0 278.9 jit_solution(10647405630408804250)
XLA Ops:
  6.5 0.0 reduce-scatter.2.cloned.1.call-start
  6.5 24.7 %while.16 = (s32[]{:T(128)}, f32[16,128,256]{2,0,1:T(8,128)}, s32[64]{0:T(128)}, s32[]{:T(128)}, bf16[64,128,128]{2,1,0:T(8,128)(2,1)}, /*index=5*/s32[64]{0:T(1...) while((s32[]{:T(128)}, f32[16,128,256]{2,0,1:T(8,128)}, ...), condition=%wide.region_2.0_spmd.clone, body=%wide.region_1.0_spmd.clone.sunk | while | flops 341314720 | bytes 24123700 | solution.py:46
  6.5 0.7 compare_select_fusion.2
  7.3 1.7 gather_fusion
  9.0 0.0 copy-start.1
  9.0 3.2 %subtract_convert_fusion.2 = (bf16[32,128,256]{2,1,0:T(8,128)(2,1)S(1)}, bf16[32,128,256]{2,1,0:T(8,128)(2,1)}) fusion(bf16[32,128,256]{2,1,0:T(8,128)(2,1)S(1)} %gather_fusion, bf16[64,128,128]{2,1,0:T(8,128)(2,1)} %get-tuple-element.322, s32[]{:T(128)S(6)} %select_n.37), kind=kOutput, calls=%fused_computation.4.clone.1 | convolution fusion | flops 272629760 | bytes 7340036 | tf_op jit(solution)/shard_map/while/body/eval_jaxpr/bij,bjk->bik/dot_general | solution.py:34
  12.2 0.0 copy-done.1
  12.2 0.1 dynamic_slice.54
  12.3 0.7 add_compare_fusion.2
  13.0 1.3 fusion.80
  14.2 4.3 %fusion.81 = f32[16,128,256]{2,0,1:T(8,128)} fusion(f32[16,128,256]{2,0,1:T(8,128)S(1)} %fusion.80, f32[16,128,256]{2,0,1:T(8,128)} %get-tuple-element.308, bf16[32,128,256]{2,1,0:T(8,128)(2,1)} %get-tuple-element.295, pred[]{:T(512)S(6)} %compare.30, s32[32]{0:T(128)S(1)} %dynamic_slice.54, pred[32]{0:T(512)(128)(4,1)S(1)} %add_compare_fusion.2), kind=kOutput, calls=%fused_computation.10.clone.1 | convolution fusion | flops 35128320 | bytes 8388769 | tf_op jit(solution)/shard_map/while/body/eval_jaxpr/mb,bik->mik/dot_general | solution.py:38
  18.6 0.7 compare_select_fusion.2
  19.3 1.7 gather_fusion
  21.0 0.0 copy-start.1
  21.0 3.2 %subtract_convert_fusion.2 = (bf16[32,128,256]{2,1,0:T(8,128)(2,1)S(1)}, bf16[32,128,256]{2,1,0:T(8,128)(2,1)}) fusion(bf16[32,128,256]{2,1,0:T(8,128)(2,1)S(1)} %gather_fusion, bf16[64,128,128]{2,1,0:T(8,128)(2,1)} %get-tuple-element.322, s32[]{:T(128)S(6)} %select_n.37), kind=kOutput, calls=%fused_computation.4.clone.1 | convolution fusion | flops 272629760 | bytes 7340036 | tf_op jit(solution)/shard_map/while/body/eval_jaxpr/bij,bjk->bik/dot_general | solution.py:34
  24.3 0.0 copy-done.1
  24.3 0.1 dynamic_slice.54
  24.3 0.7 add_compare_fusion.2
  25.0 1.3 fusion.80
  26.3 5.0 %fusion.81 = f32[16,128,256]{2,0,1:T(8,128)} fusion(f32[16,128,256]{2,0,1:T(8,128)S(1)} %fusion.80, f32[16,128,256]{2,0,1:T(8,128)} %get-tuple-element.308, bf16[32,128,256]{2,1,0:T(8,128)(2,1)} %get-tuple-element.295, pred[]{:T(512)S(6)} %compare.30, s32[32]{0:T(128)S(1)} %dynamic_slice.54, pred[32]{0:T(512)(128)(4,1)S(1)} %add_compare_fusion.2), kind=kOutput, calls=%fused_computation.10.clone.1 | convolution fusion | flops 35128320 | bytes 8388769 | tf_op jit(solution)/shard_map/while/body/eval_jaxpr/mb,bik->mik/dot_general | solution.py:38
  31.2 4.1 %copy.18 = f32[16,128,256]{2,1,0:T(8,128)} copy(f32[16,128,256]{2,0,1:T(8,128)} %get-tuple-element.144) | data formatting | bytes 4194304 | tf_op jit(solution)/shard_map/while | solution.py:46
  35.3 0.0 reduce-scatter.2.cloned.1.call-update
  35.4 0.0 all-reduce.3.cloned.1.call-start
  35.4 0.9 convert_reduce_fusion
  36.4 37.0 %reduce-scatter.2.cloned.1.call-done = f32[512,256]{1,0:T(8,128)} async-done(((f32[2048,256]{1,0:T(8,128)}), f32[512,256]{1,0:T(8,128)}) %reduce-scatter.2.cloned.1.call-update) | async-done | bytes 524304 | tf_op jit(solution)/shard_map/reduce_scatter | solution.py:53
  73.4 1.3 reduce_sum.19
  74.7 0.8 subtract_divide_fusion.1
  75.5 3.2 %fusion.54 = f32[256,256]{0,1:T(8,128)} fusion(f32[512,256]{1,0:T(8,128)} %reduce-scatter.2.cloned.1.call-done, f32[512]{0:T(512)S(1)} %get-tuple-element.216, f32[512]{0:T(512)S(1)} %get-tuple-element.217), kind=kOutput, calls=%fused_computation.89 | convolution fusion | flops 402915328 | bytes 790528 | tf_op jit(solution)/shard_map/dot_general | solution.py:59
  78.7 0.0 all-reduce.3.cloned.1.call-update
  78.7 0.0 copy-done
  78.7 0.4 fusion.53
  79.2 39.5 %psum.15 = f32[256]{0:T(256)S(1)} all-reduce(f32[256]{0:T(256)S(1)} %bitcast.108), channel_id=1, replica_groups=mesh['obs'=8,'state'=4] {'obs','state'}, use_global_device_ids=true, to_apply=%region_10.11 | all-reduce | flops 256 | bytes 2048 | tf_op jit(solution)/shard_map/psum | solution.py:64
  118.6 87.0 %all-reduce.3.cloned.1.call-done = f32[256,256]{0,1:T(8,128)} async-done(((f32[256,256]{0,1:T(8,128)}), f32[256,256]{0,1:T(8,128)}) %all-reduce.3.cloned.1.call-update) | async-done | bytes 262160 | tf_op jit(solution)/shard_map/psum | solution.py:64
  205.6 1.0 select_add_fusion.1
  206.6 0.1 copy.20
  206.7 1.0 fusion.28
  207.7 11.7 %cholesky.49 = f32[128,128]{1,0:T(8,128)S(1)} custom-call(f32[128,128]{1,0:T(8,128)S(1)} %cholesky.115), custom_call_target="Cholesky" | custom-call | tf_op jit(solution)/shard_map/jit(cholesky)/cholesky | solution.py:65
  219.5 9.8 %custom-call.18 = f32[1,128,128]{1,2,0:T(8,128)S(1)} custom-call(f32[1,128,128]{2,1,0:T(8,128)S(1)} %get-tuple-element.214), custom_call_target="InvertDiagBlocksLowerTriangular" | custom-call | tf_op jit(solution)/shard_map/jit(cholesky)/cholesky | solution.py:65
  229.3 0.2 fusion.37
  229.5 0.3 convolution_subtract_fusion.1
  229.8 11.7 %cholesky.103 = f32[128,128]{1,0:T(8,128)S(1)} custom-call(f32[128,128]{1,0:T(8,128)S(1)} %convolution_subtract_fusion.1), custom_call_target="Cholesky" | custom-call | tf_op jit(solution)/shard_map/jit(cholesky)/cholesky | solution.py:65
  241.5 0.1 copy.23
  241.6 0.1 copy.22
  241.7 0.1 copy.21
  241.9 0.7 compare_reduce_fusion
  243.9 0.1 triangular_solve.94
  244.0 4.3 %while.15 = (s32[]{:T(128)}, f32[256,256]{0,1:T(8,128)S(1)}, s32[2,2]{1,0:T(2,128)S(1)}, f32[2,128,128]{2,1,0:T(8,128)S(1)}, s32[]{:T(128)}) while((s32[]{:T(128)}, f32[256,256]{0,1:T(8,128)S(1)}, s32[2,2]{1,0:T(2,128)S(1)}, f32[2,128,128]{2,1,0:T(8,128)S(1)}, s32[]{:T(128)}) %tuple.58), condition=%wide.while_cond, body=%wide.while_body.sunk | while | flops 2 | bytes 393321 | solution.py:72
  244.0 0.7 fusion.74
  244.6 1.3 dynamic-slice.8
  246.0 0.1 copy.36
  246.1 0.7 fusion.74
  246.8 1.3 dynamic-slice.8
  248.1 0.1 copy.36
  248.3 19.9 %custom-call.19 = f32[2,128,128]{1,2,0:T(8,128)S(1)} custom-call(f32[2,128,128]{2,1,0:T(8,128)S(1)} %get-tuple-element.152), custom_call_target="InvertDiagBlocksLowerTriangular" | custom-call | tf_op jit(solution)/shard_map/triangular_solve | solution.py:72
  268.2 0.2 fusion.41
  268.3 0.2 fusion.25
  268.5 0.2 convolution_bitcast_fusion.3
  268.7 0.2 convolution_bitcast_fusion.2
  268.9 0.2 fusion.23
  269.1 0.2 convolution_bitcast_fusion
  269.3 0.3 fusion.34
  269.6 0.4 convolution_subtract_fusion
  270.0 0.3 fusion.42
  270.3 1.7 fusion.21
  (20 shorter events, 0.2 us)
Async XLA Ops:
  6.5 66.9 %reduce-scatter.2.cloned.1.call-start = ((), (), s32[]{:S(2)}) async-start(), calls=%async_computation.1 | async-start | bytes 2621440 | tf_op jit(solution)/shard_map/reduce_scatter | solution.py:53
  9.0 3.2 %copy-start.1 = (s32[64]{0:T(128)S(1)}, s32[64]{0:T(128)}, u32[]{:S(2)}) copy-start(s32[64]{0:T(128)} %get-tuple-element.320) | copy-start | bytes 772 | tf_op jit(solution)/shard_map/while
  21.0 3.2 %copy-start.1 = (s32[64]{0:T(128)S(1)}, s32[64]{0:T(128)}, u32[]{:S(2)}) copy-start(s32[64]{0:T(128)} %get-tuple-element.320) | copy-start | bytes 772 | tf_op jit(solution)/shard_map/while
  35.4 170.3 %all-reduce.3.cloned.1.call-start = ((), (), s32[]{:S(2)}) async-start(), calls=%async_computation.2 | async-start | bytes 524288 | tf_op jit(solution)/shard_map/psum | solution.py:64
  73.4 5.3 %copy-start = (f32[512,256]{1,0:T(8,128)S(1)}, f32[512,256]{1,0:T(8,128)}, u32[]{:S(2)}) copy-start(f32[512,256]{1,0:T(8,128)} %reduce-scatter.2.cloned.1.call-done) | copy-start | bytes 1572868
Sparse Core Ops, SparseCore 0:
  35.5 37.9 reduce-scatter.1
  78.9 126.6 all-reduce.2
where the time goes:
time: 280 us; the launch traced here: 279 us
  waiting for transfers between devices  124 us (44%)
  other arithmetic  61.7 us (22%)
  blocking collectives  39.5 us (14%)
  matrix products  26.2 us (9%)
  between operations  14.9 us (5%)
  local copies, waits for them, and re-layouts  12.4 us (4%)
    psum x1, waiting for transfers between devices, on_device(): lax.psum((gram_part, projected_part), ('obs', 'state'))  87 us
    psum x1, blocking collectives, on_device(): lax.psum((gram_part, projected_part), ('obs', 'state'))  39.5 us
    reduce_scatter x1, waiting for transfers between devices, on_device(): lax.psum_scatter(slab_term, 'state', scatter_dimension=0, tiled=True)  37 us
    another operation x6, other arithmetic, on_device(): lower_factor = jnp.linalg.cholesky(gram_sum + (K - 1) * identity)  34 us
    another operation x3, other arithmetic, on_device(): lax.linalg.triangular_solve(lower_factor, identity, left_side=True, lower...  19.9 us
    dot_general x2, matrix products, add_group(): jnp.einsum('mb,bik->mik', onehot, upper_part, preferred_element_type=jnp....  9.29 us
    dot_general x2, matrix products, add_group(): jnp.einsum('bij,bjk->bik', blocks, picked, preferred_element_type=jnp.flo...  6.45 us
  transfers between devices with their start and end apart: 2, of which 2 were waited for; matrix products, arithmetic and copies ran while one was open for 1% of the time, Pallas kernels for 0%

commit v1 on v0

--- a/solution.py
+++ b/solution.py
@@ -61,7 +61,10 @@
     )
     projected_part = jnp.dot(innovation, whitened, precision=lax.Precision.HIGHEST)
     identity = jnp.eye(K, dtype=jnp.float32)
-    gram_sum, projected_innovation = lax.psum((gram_part, projected_part), ("obs", "state"))
+    _change_quarters = lambda target, dev_axis, comm_axis: lax.psum(
+        lax.psum(target, axis_name=dev_axis), axis_name=comm_axis
+    )
+    gram_sum, projected_innovation = _change_quarters((gram_part, projected_part), "state", "obs")
     lower_factor = jnp.linalg.cholesky(gram_sum + (K - 1) * identity)
     halfway = lax.linalg.triangular_solve(
         lower_factor, projected_innovation[:, None], left_side=True, lower=True

time: 280 us -> 253 us (0.904)
  blocking collectives: 39.5 us -> 23 us
  waiting for transfers between devices: 124 us -> 115 us
    psum x1 -> x2, blocking collectives: 39.5 us -> 23 us  [the longest x1 14.1 us: on_device(): lax.psum(lax.psum(target, axis_name=dev_axis), axis_name=comm_axis)]
    psum x1 -> x2, waiting for transfers between devices: 87 us -> 76.5 us  [the longest x1 42.2 us: on_device(): lax.psum(target, axis_name=dev_axis)]
  transfers between devices with their start and end apart: 2 -> 3, of which waited for: 2 -> 3; matrix products, arithmetic and copies ran while one was open for 1% -> 1% of each run, Pallas kernels for 0% -> 0%
where the time goes in v1:
time: 253 us
  waiting for transfers between devices  115 us (45%)
  other arithmetic  61.7 us (24%)
  matrix products  26.2 us (10%)
  blocking collectives  23 us (9%)
  between operations  14.6 us (6%)
  local copies, waits for them, and re-layouts  12.4 us (5%)
    psum x1, waiting for transfers between devices, on_device(): lax.psum(target, axis_name=dev_axis)  42.2 us
    reduce_scatter x1, waiting for transfers between devices, on_device(): lax.psum_scatter(slab_term, 'state', scatter_dimension=0, tiled=True)  38 us
    psum x1, waiting for transfers between devices, on_device(): lax.psum(lax.psum(target, axis_name=dev_axis), axis_name=comm_axis)  34.3 us
    another operation x6, other arithmetic, on_device(): lower_factor = jnp.linalg.cholesky(gram_sum + (K - 1) * identity)  34 us
    another operation x3, other arithmetic, on_device(): lax.linalg.triangular_solve(lower_factor, identity, left_side=True, lower...  19.9 us
    psum x1, blocking collectives, on_device(): lax.psum(lax.psum(target, axis_name=dev_axis), axis_name=comm_axis)  14.1 us
    dot_general x2, matrix products, add_group(): jnp.einsum('mb,bik->mik', onehot, upper_part, preferred_element_type=jnp....  9.29 us
    psum x1, blocking collectives, on_device(): lax.psum(target, axis_name=dev_axis)  8.96 us
  transfers between devices with their start and end apart: 3, of which 3 were waited for; matrix products, arithmetic and copies ran while one was open for 1% of the time, Pallas kernels for 0%

profile of v1, /device:TPU:0, one launch (start us, length us, event | category | flops | bytes accessed | tf_op | source)
XLA Modules:
  0.0 252.7 jit_solution(10752231702190541496)
XLA Ops:
  6.5 24.7 %while.16 = (s32[]{:T(128)}, f32[16,128,256]{2,0,1:T(8,128)}, s32[64]{0:T(128)}, s32[]{:T(128)}, bf16[64,128,128]{2,1,0:T(8,128)(2,1)}, /*index=5*/s32[64]{0:T(1...) while((s32[]{:T(128)}, f32[16,128,256]{2,0,1:T(8,128)}, ...), condition=%wide.region_2.0_spmd.clone, body=%wide.region_1.0_spmd.clone.sunk | while | flops 341314720 | bytes 24123700 | solution.py:46
  6.5 0.7 compare_select_fusion.2
  7.3 1.7 gather_fusion
  9.0 0.0 copy-start.1
  9.0 3.2 %subtract_convert_fusion.2 = (bf16[32,128,256]{2,1,0:T(8,128)(2,1)S(1)}, bf16[32,128,256]{2,1,0:T(8,128)(2,1)}) fusion(bf16[32,128,256]{2,1,0:T(8,128)(2,1)S(1)} %gather_fusion, bf16[64,128,128]{2,1,0:T(8,128)(2,1)} %get-tuple-element.322, s32[]{:T(128)S(6)} %select_n.37), kind=kOutput, calls=%fused_computation.4.clone.1 | convolution fusion | flops 272629760 | bytes 7340036 | tf_op jit(solution)/shard_map/while/body/eval_jaxpr/bij,bjk->bik/dot_general | solution.py:34
  12.2 0.1 dynamic_slice.54
  12.3 0.7 add_compare_fusion.2
  13.0 1.3 fusion.80
  14.2 4.3 %fusion.81 = f32[16,128,256]{2,0,1:T(8,128)} fusion(f32[16,128,256]{2,0,1:T(8,128)S(1)} %fusion.80, f32[16,128,256]{2,0,1:T(8,128)} %get-tuple-element.308, bf16[32,128,256]{2,1,0:T(8,128)(2,1)} %get-tuple-element.295, pred[]{:T(512)S(6)} %compare.30, s32[32]{0:T(128)S(1)} %dynamic_slice.54, pred[32]{0:T(512)(128)(4,1)S(1)} %add_compare_fusion.2), kind=kOutput, calls=%fused_computation.10.clone.1 | convolution fusion | flops 35128320 | bytes 8388769 | tf_op jit(solution)/shard_map/while/body/eval_jaxpr/mb,bik->mik/dot_general | solution.py:38
  18.6 0.7 compare_select_fusion.2
  19.3 1.7 gather_fusion
  21.0 0.0 copy-start.1
  21.0 3.2 %subtract_convert_fusion.2 = (bf16[32,128,256]{2,1,0:T(8,128)(2,1)S(1)}, bf16[32,128,256]{2,1,0:T(8,128)(2,1)}) fusion(bf16[32,128,256]{2,1,0:T(8,128)(2,1)S(1)} %gather_fusion, bf16[64,128,128]{2,1,0:T(8,128)(2,1)} %get-tuple-element.322, s32[]{:T(128)S(6)} %select_n.37), kind=kOutput, calls=%fused_computation.4.clone.1 | convolution fusion | flops 272629760 | bytes 7340036 | tf_op jit(solution)/shard_map/while/body/eval_jaxpr/bij,bjk->bik/dot_general | solution.py:34
  24.3 0.1 dynamic_slice.54
  24.3 0.7 add_compare_fusion.2
  25.0 1.3 fusion.80
  26.3 5.0 %fusion.81 = f32[16,128,256]{2,0,1:T(8,128)} fusion(f32[16,128,256]{2,0,1:T(8,128)S(1)} %fusion.80, f32[16,128,256]{2,0,1:T(8,128)} %get-tuple-element.308, bf16[32,128,256]{2,1,0:T(8,128)(2,1)} %get-tuple-element.295, pred[]{:T(512)S(6)} %compare.30, s32[32]{0:T(128)S(1)} %dynamic_slice.54, pred[32]{0:T(512)(128)(4,1)S(1)} %add_compare_fusion.2), kind=kOutput, calls=%fused_computation.10.clone.1 | convolution fusion | flops 35128320 | bytes 8388769 | tf_op jit(solution)/shard_map/while/body/eval_jaxpr/mb,bik->mik/dot_general | solution.py:38
  31.2 4.1 %copy.18 = f32[16,128,256]{2,1,0:T(8,128)} copy(f32[16,128,256]{2,0,1:T(8,128)} %get-tuple-element.144) | data formatting | bytes 4194304 | tf_op jit(solution)/shard_map/while | solution.py:46
  35.3 0.0 reduce-scatter.2.cloned.1.call-update
  35.4 0.0 all-reduce.4.cloned.1.call-start
  35.4 38.0 %reduce-scatter.2.cloned.1.call-done = f32[512,256]{1,0:T(8,128)} async-done(((f32[2048,256]{1,0:T(8,128)}), f32[512,256]{1,0:T(8,128)}) %reduce-scatter.2.cloned.1.call-update) | async-done | bytes 524304 | tf_op jit(solution)/shard_map/reduce_scatter | solution.py:53
  73.4 1.3 reduce_sum.19
  74.7 0.8 subtract_divide_fusion.1
  75.5 3.2 %fusion.54 = f32[256,256]{0,1:T(8,128)} fusion(f32[512,256]{1,0:T(8,128)} %reduce-scatter.2.cloned.1.call-done, f32[512]{0:T(512)S(1)} %get-tuple-element.216, f32[512]{0:T(512)S(1)} %get-tuple-element.217), kind=kOutput, calls=%fused_computation.89 | convolution fusion | flops 402915328 | bytes 790528 | tf_op jit(solution)/shard_map/dot_general | solution.py:59
  78.7 0.0 all-reduce.4.cloned.1.call-update
  78.7 0.0 all-reduce.6.cloned.1.call-start
  78.8 0.9 convert_reduce_fusion
  79.8 42.2 %all-reduce.4.cloned.1.call-done = f32[256,256]{0,1:T(8,128)} async-done(((f32[256,256]{0,1:T(8,128)}), f32[256,256]{0,1:T(8,128)}) %all-reduce.4.cloned.1.call-update) | async-done | bytes 262160 | tf_op jit(solution)/shard_map/psum | solution.py:65
  121.9 0.0 all-reduce.6.cloned.1.call-update
  122.0 0.4 fusion.53
  122.4 9.0 %psum.30 = f32[256]{0:T(256)S(1)} all-reduce(f32[256]{0:T(256)S(1)} %bitcast.108), channel_id=1, replica_groups=mesh['obs'=8,'state'=4] {'state'}, use_global_device_ids=true, to_apply=%region_11.12 | all-reduce | flops 256 | bytes 2048 | tf_op jit(solution)/shard_map/psum | solution.py:65
  131.4 14.1 %psum.31 = f32[256]{0:T(256)S(1)} all-reduce(f32[256]{0:T(256)S(1)} %psum.30), channel_id=1, replica_groups=mesh['obs'=8,'state'=4] {'obs'}, use_global_device_ids=true, to_apply=%region_12.13 | all-reduce | flops 256 | bytes 2048 | tf_op jit(solution)/shard_map/psum | solution.py:64
  145.4 34.3 %all-reduce.6.cloned.1.call-done = f32[256,256]{0,1:T(8,128)} async-done(((f32[256,256]{0,1:T(8,128)}), f32[256,256]{0,1:T(8,128)}) %all-reduce.6.cloned.1.call-update) | async-done | bytes 262160 | tf_op jit(solution)/shard_map/psum | solution.py:64
  179.7 1.0 select_add_fusion.1
  180.7 0.1 copy.20
  180.9 1.0 fusion.28
  181.9 11.7 %cholesky.49 = f32[128,128]{1,0:T(8,128)S(1)} custom-call(f32[128,128]{1,0:T(8,128)S(1)} %cholesky.115), custom_call_target="Cholesky" | custom-call | tf_op jit(solution)/shard_map/jit(cholesky)/cholesky | solution.py:68
  193.6 9.8 %custom-call.18 = f32[1,128,128]{1,2,0:T(8,128)S(1)} custom-call(f32[1,128,128]{2,1,0:T(8,128)S(1)} %get-tuple-element.214), custom_call_target="InvertDiagBlocksLowerTriangular" | custom-call | tf_op jit(solution)/shard_map/jit(cholesky)/cholesky | solution.py:68
  203.4 0.2 fusion.37
  203.6 0.3 convolution_subtract_fusion.1
  203.9 11.7 %cholesky.103 = f32[128,128]{1,0:T(8,128)S(1)} custom-call(f32[128,128]{1,0:T(8,128)S(1)} %convolution_subtract_fusion.1), custom_call_target="Cholesky" | custom-call | tf_op jit(solution)/shard_map/jit(cholesky)/cholesky | solution.py:68
  215.7 0.1 copy.23
  215.8 0.1 copy.22
  215.9 0.1 copy.21
  216.0 0.7 compare_reduce_fusion
  218.0 0.1 triangular_solve.94
  218.1 4.3 %while.15 = (s32[]{:T(128)}, f32[256,256]{0,1:T(8,128)S(1)}, s32[2,2]{1,0:T(2,128)S(1)}, f32[2,128,128]{2,1,0:T(8,128)S(1)}, s32[]{:T(128)}) while((s32[]{:T(128)}, f32[256,256]{0,1:T(8,128)S(1)}, s32[2,2]{1,0:T(2,128)S(1)}, f32[2,128,128]{2,1,0:T(8,128)S(1)}, s32[]{:T(128)}) %tuple.58), condition=%wide.while_cond, body=%wide.while_body.sunk | while | flops 2 | bytes 393321 | solution.py:75
  218.1 0.7 fusion.74
  218.8 1.3 dynamic-slice.8
  220.1 0.1 copy.36
  220.3 0.7 fusion.74
  220.9 1.3 dynamic-slice.8
  222.3 0.1 copy.36
  222.4 19.9 %custom-call.19 = f32[2,128,128]{1,2,0:T(8,128)S(1)} custom-call(f32[2,128,128]{2,1,0:T(8,128)S(1)} %get-tuple-element.152), custom_call_target="InvertDiagBlocksLowerTriangular" | custom-call | tf_op jit(solution)/shard_map/triangular_solve | solution.py:75
  242.3 0.2 fusion.41
  242.5 0.2 fusion.25
  242.6 0.2 convolution_bitcast_fusion.3
  242.8 0.2 convolution_bitcast_fusion.2
  243.0 0.2 fusion.23
  243.2 0.2 convolution_bitcast_fusion
  243.4 0.3 fusion.34
  243.7 0.4 convolution_subtract_fusion
  244.1 0.3 fusion.42
  244.4 1.7 fusion.21
  (24 shorter events, 0.3 us)
Async XLA Ops:
  6.5 66.9 %reduce-scatter.2.cloned.1.call-start = ((), (), s32[]{:S(2)}) async-start(), calls=%async_computation.1 | async-start | bytes 2621440 | tf_op jit(solution)/shard_map/reduce_scatter | solution.py:53
  9.0 3.2 %copy-start.1 = (s32[64]{0:T(128)S(1)}, s32[64]{0:T(128)}, u32[]{:S(2)}) copy-start(s32[64]{0:T(128)} %get-tuple-element.320) | copy-start | bytes 772 | tf_op jit(solution)/shard_map/while
  21.0 3.2 %copy-start.1 = (s32[64]{0:T(128)S(1)}, s32[64]{0:T(128)}, u32[]{:S(2)}) copy-start(s32[64]{0:T(128)} %get-tuple-element.320) | copy-start | bytes 772 | tf_op jit(solution)/shard_map/while
  35.4 86.6 %all-reduce.4.cloned.1.call-start = ((), (), s32[]{:S(2)}) async-start(), calls=%async_computation.2 | async-start | bytes 524288 | tf_op jit(solution)/shard_map/psum | solution.py:65
  73.4 48.5 %copy-start = (f32[512,256]{1,0:T(8,128)S(1)}, f32[512,256]{1,0:T(8,128)}, u32[]{:S(2)}) copy-start(f32[512,256]{1,0:T(8,128)} %reduce-scatter.2.cloned.1.call-done) | copy-start | bytes 1572868
  78.7 101.0 %all-reduce.6.cloned.1.call-start = ((), (), s32[]{:S(2)}) async-start(), calls=%async_computation.3 | async-start | bytes 524288 | tf_op jit(solution)/shard_map/psum | solution.py:64
Sparse Core Ops, SparseCore 0:
  35.5 37.9 reduce-scatter.1
  78.9 43.0 all-reduce.3
  124.3 55.4 all-reduce.5
